TPU v7x, 256 devices: a whole 4x4x8 slice. The times are simulated.
256 devices in a mesh: dp: 8 (over y, core), expert: 32 (over x, z).
Axes of the slice: x: 4, y: 4, z: 8, core: 2. Of those that a mesh axis runs over, the one named last changes fastest.
Arguments:
- tokens: bfloat16 [32768, 2048], P(('dp', 'expert')), may hold values from -6 to 6
- expert_ids: int32 [32768, 2], P(('dp', 'expert')), may hold values from 0 to 31, all different within a row; in each aligned block of 128 rows (0 to 127, 128 to 255, ...) at most 12 rows name the same one
- upstream: bfloat16 [32768, 2048], P(('dp', 'expert')), may hold values from -6 to 6
- gain: float32 [2048], replicated, may hold values from 0.5 to 1.5
- router: bfloat16 [2048, 32], replicated, may hold values from -0.125 to 0.125
- gate_weight_matrix: bfloat16 [32, 2048, 1024], P('expert', 'dp'), may hold values from -0.125 to 0.125
- up_weight: bfloat16 [32, 2048, 1024], P('expert', 'dp'), may hold values from -0.125 to 0.125
- down_weight: bfloat16 [32, 1024, 2048], P('expert', None, 'dp'), may hold values from -0.1875 to 0.1875
Outputs:
- mixed: bfloat16 [32768, 2048], P(('dp', 'expert'))
- d_tokens: bfloat16 [32768, 2048], P(('dp', 'expert'))
- gate_weight_gradient: bfloat16 [32, 2048, 1024], P('expert', 'dp')
- up_weight_gradient: bfloat16 [32, 2048, 1024], P('expert', 'dp')
- down_weight_gradient: bfloat16 [32, 1024, 2048], P('expert', None, 'dp')
- d_router: float32 [2048, 32], replicated
- d_gain: float32 [2048], replicated
Inputs may be any that keep to these rules, and one draw needn't show every extreme that they name: `expert_ids`: the two experts of a token differ. Among the tokens of one device (aligned blocks of 128 rows) no expert is named more than 12 times, and in some block one expert is named exactly 12 times.
All inputs are finite; a program needn't handle non-finite values.
Results may differ from a plain program's by a relative error of at most 0.014.
Values may be sent and summed in bfloat16 or wider, within the bound.
No kernel may reach another device: no remote copies, remote signals or barrier semaphores. Data moves between devices by JAX's collectives and lax.ppermute only.
A program may use at most 128 MiB of HBM per device.

v0:
```python
import jax
import jax.numpy as jnp
from jax import lax
from jax.sharding import PartitionSpec as P

norm_eps = 1e-06


def slot_layout(expert_ids, experts, capacity):
    flattened = expert_ids.reshape(-1)
    onehot = (flattened[:, None] == jnp.arange(experts, dtype=jnp.int32)[None, :]).astype(jnp.int32)
    ranking = jnp.sum(jnp.cumsum(onehot, axis=0) * onehot, axis=1) - 1
    slot_ids = flattened * capacity + ranking
    sources = (
        jnp.zeros((experts * capacity,), jnp.int32)
        .at[slot_ids]
        .set(jnp.arange(flattened.shape[0], dtype=jnp.int32))
    )
    counts = jnp.sum(onehot, axis=0)
    slots_occupied = (jnp.arange(capacity, dtype=jnp.int32)[None, :] < counts[:, None]).reshape(-1)
    return (slot_ids, sources, slots_occupied)


def transposed_product(left, right):
    return lax.dot_general(
        left, right, (((1,), (1,)), ((), ())), preferred_element_type=jnp.float32
    )


def inner_product(left, right):
    return lax.dot_general(
        left, right, (((0,), (0,)), ((), ())), preferred_element_type=jnp.float32
    )


def on_device(
    tokens, expert_ids, upstream, gain, router, gate_weight_matrix, up_weight, down_weight
):
    experts = lax.axis_size("expert")
    tok_rows = tokens.shape[0]
    width = tokens.shape[1]
    feed = gate_weight_matrix.shape[2]
    capacity = 3 * tok_rows // experts
    source = tokens.astype(jnp.float32)
    inverse = lax.rsqrt(jnp.mean(source * source, axis=-1, keepdims=True) + norm_eps)
    unit_rows = source * inverse
    normed = (unit_rows * gain).astype(jnp.bfloat16)
    scores = jax.nn.sigmoid(jnp.dot(normed, router, preferred_element_type=jnp.float32))
    picked = expert_ids[:, :, None] == jnp.arange(experts, dtype=jnp.int32)[None, None, :]
    chosen = jnp.sum(jnp.where(picked, scores[:, None, :], 0.0), axis=2)
    total = jnp.sum(chosen, axis=1, keepdims=True)
    gates = chosen / total
    slot_ids, sources, slots_occupied = slot_layout(expert_ids, experts, capacity)
    slot_pairs = slot_ids.reshape(tok_rows, 2)
    send_rows = jnp.where(
        slots_occupied[:, None], normed[sources // 2], jnp.zeros((), jnp.bfloat16)
    )
    arrived = lax.all_to_all(
        send_rows.reshape(experts, capacity, width),
        "expert",
        split_axis=0,
        concat_axis=0,
        tiled=True,
    )
    expert_in = arrived.reshape(experts * capacity, width)
    pieces = (
        lax.all_gather(gate_weight_matrix, "dp", axis=1, tiled=True),
        lax.all_gather(up_weight, "dp", axis=1, tiled=True),
    )
    columns = expert_in
    pre_gate = jnp.dot(columns, pieces[0][0], preferred_element_type=jnp.float32)
    pre_up = jnp.dot(columns, pieces[1][0], preferred_element_type=jnp.float32)
    sigma = jax.nn.sigmoid(pre_gate)
    active = pre_gate * sigma
    hidden = (active * pre_up).astype(jnp.bfloat16)
    expert_out = jnp.dot(
        hidden,
        lax.all_gather(down_weight, "dp", axis=2, tiled=True)[0],
        preferred_element_type=jnp.float32,
    ).astype(jnp.bfloat16)
    returned = lax.all_to_all(
        expert_out.reshape(experts, capacity, width),
        "expert",
        split_axis=0,
        concat_axis=0,
        tiled=True,
    )
    outputs = returned.reshape(experts * capacity, width)[slot_pairs].astype(jnp.float32)
    combined = gates[:, :, None] * outputs
    mixed = (source + combined[:, 0] + combined[:, 1]).astype(jnp.bfloat16)
    cotangent = upstream.astype(jnp.float32)
    d_gates = jnp.sum(cotangent[:, None, :] * outputs, axis=2)
    weight_rows = gates.reshape(-1)[sources]
    d_send = jnp.where(
        slots_occupied[:, None], weight_rows[:, None] * cotangent[sources // 2], 0.0
    ).astype(jnp.bfloat16)
    d_arrived = lax.all_to_all(
        d_send.reshape(experts, capacity, width), "expert", split_axis=0, concat_axis=0, tiled=True
    )
    d_out = d_arrived.reshape(experts * capacity, width)
    columns = d_out
    d_hidden = transposed_product(columns, lax.all_gather(down_weight, "dp", axis=2, tiled=True)[0])
    d_pre_gate = (d_hidden * pre_up * sigma * (1.0 + pre_gate * (1.0 - sigma))).astype(jnp.bfloat16)
    d_pre_up = (d_hidden * active).astype(jnp.bfloat16)
    pieces = (
        lax.all_gather(gate_weight_matrix, "dp", axis=1, tiled=True),
        lax.all_gather(up_weight, "dp", axis=1, tiled=True),
    )
    block = transposed_product(d_pre_gate, pieces[0][0]) + transposed_product(
        d_pre_up, pieces[1][0]
    )
    d_rows = block.astype(jnp.bfloat16)
    d_back = lax.all_to_all(
        d_rows.reshape(experts, capacity, width), "expert", split_axis=0, concat_axis=0, tiled=True
    )
    d_parts = d_back.reshape(experts * capacity, width)[slot_pairs].astype(jnp.float32)
    grad_rows = lax.psum_scatter(
        jnp.concatenate(
            [
                inner_product(expert_in, d_pre_gate),
                inner_product(expert_in, d_pre_up),
                inner_product(d_out, hidden),
            ],
            axis=1,
        ).astype(jnp.bfloat16),
        "dp",
        scatter_dimension=0,
        tiled=True,
    ).astype(jnp.float32)
    gate_weight_gradient = grad_rows[:, :feed].astype(jnp.bfloat16)[None]
    up_weight_gradient = grad_rows[:, feed : 2 * feed].astype(jnp.bfloat16)[None]
    down_weight_gradient = grad_rows[:, 2 * feed :].T.astype(jnp.bfloat16)[None]
    blended = jnp.sum(gates * d_gates, axis=1, keepdims=True)
    d_chosen = (d_gates - blended) / total
    d_logit = d_chosen * chosen * (1.0 - chosen)
    d_logits = jnp.sum(jnp.where(picked, d_logit[:, :, None], 0.0), axis=1)
    router_float = router.astype(jnp.float32)
    d_normed = (
        d_parts[:, 0]
        + d_parts[:, 1]
        + jnp.dot(d_logits, router_float.T, precision=lax.Precision.HIGHEST)
    )
    d_unit = d_normed * gain
    inner = jnp.mean(d_unit * unit_rows, axis=-1, keepdims=True)
    d_tokens = (cotangent + inverse * (d_unit - unit_rows * inner)).astype(jnp.bfloat16)
    part_router = jnp.dot(normed.astype(jnp.float32).T, d_logits, precision=lax.Precision.HIGHEST)
    part_gain = jnp.sum(d_normed * unit_rows, axis=0)
    d_router, d_gain = lax.psum((part_router, part_gain), ("dp", "expert"))
    return (
        mixed,
        d_tokens,
        gate_weight_gradient,
        up_weight_gradient,
        down_weight_gradient,
        d_router,
        d_gain,
    )


def solution(mesh):
    return jax.shard_map(
        on_device,
        mesh=mesh,
        in_specs=(
            P(("dp", "expert"), None),
            P(("dp", "expert"), None),
            P(("dp", "expert"), None),
            P(),
            P(),
            P("expert", "dp", None),
            P("expert", "dp", None),
            P("expert", None, "dp"),
        ),
        out_specs=(
            P(("dp", "expert"), None),
            P(("dp", "expert"), None),
            P("expert", "dp", None),
            P("expert", "dp", None),
            P("expert", None, "dp"),
            P(),
            P(),
        ),
        check_vma=False,
    )
```

profile of v0, /device:TPU:2, one launch (start us, length us, event | category | flops | bytes accessed | tf_op | source)
XLA Modules:
  0.0 638.8 jit_solution(4836383149556349928)
XLA Ops:
  7.3 0.7 all-gather.4.cloned.1.call-update
  8.0 0.7 all-gather.6.cloned.1.call-update
  8.7 0.7 all-gather.8.cloned.1.call-update
  9.4 0.8 copy.42
  10.2 0.1 eq.45
  10.4 0.1 eq.41
  10.5 0.6 reduce-window.6
  11.1 0.2 slice_reduce_fusion
  11.3 0.2 convert_reduce_fusion
  11.5 0.1 sub.47
  11.7 0.1 mul.138
  11.8 1.4 scatter_custom_fusion
  13.3 0.2 fusion.32
  13.5 0.2 fusion.25
  13.7 3.1 gather_fusion
  16.8 2.4 gather.20
  19.2 0.2 broadcast_select_fusion
  19.5 60.0 %all_to_all.20 = bf16[32,12,2048]{2,1,0:T(8,128)(2,1)S(1)} all-to-all(bf16[32,12,2048]{2,1,0:T(8,128)(2,1)S(1)} %broadcast_select_fusion), channel_id=1, replica_groups=mesh['dp'=8,'expert'=32] {'expert'}, dimensions={0} | all-to-all | bytes 3145728 | tf_op jit(solution)/shard_map/all_to_all | solution.py:58
  79.4 1.4 reshape.196
  80.9 5.8 fusion.10
  86.6 5.9 multiply_convert_fusion.2
  92.6 31.3 %all-gather.8.cloned.1.call-done = bf16[1,1024,2048]{2,1,0:T(8,128)(2,1)} async-done(((bf16[1,1024,256]{2,1,0:T(8,128)(2,1)}), bf16[1,1024,2048]{2,1,0:T(8,128)(2,1)}) %all-gather.8.cloned.1.call-update) | async-done | bytes 4194320 | tf_op jit(solution)/shard_map/all_gather | solution.py:78
  123.9 4.2 fusion.14
  128.1 1.6 reshape.197
  129.7 10.3 %all-to-all-start.1 = ((bf16[32,12,2048]{2,1,0:T(8,128)(2,1)}), bf16[32,12,2048]{2,1,0:T(8,128)(2,1)}, u32[]{:S(2)}, u32[]{:S(2)}) async-start(bf16[32,12,2048]{2,1,0:T(8,128)(2,1)} %reshape.197), calls=%async_computation.1 | async-start | bytes 4194304 | tf_op jit(solution)/shard_map/all_to_all | solution.py:81
  140.0 0.3 reduce-scatter.2.cloned.1.call-start
  140.6 3.3 gather_fusion.3
  143.9 4.6 gather.24
  148.5 0.3 fusion.24
  148.9 39.2 %all-to-all-done.1 = bf16[32,12,2048]{2,1,0:T(8,128)(2,1)} async-done(((bf16[32,12,2048]{2,1,0:T(8,128)(2,1)}), bf16[32,12,2048]{2,1,0:T(8,128)(2,1)}, u32[]{:S(2)}, u32[]{:S(2)}) %all-to-all-start.1) | async-done | bytes 1572896 | tf_op jit(solution)/shard_map/all_to_all | solution.py:81
  188.1 2.5 reshape.198
  190.6 2.4 gather_fusion.1
  193.0 3.4 reshape.257
  196.3 2.6 multiply_reduce_fusion
  199.2 0.1 div.58
  199.3 2.8 gather_fusion.2
  202.2 2.6 select_convert_fusion
  204.9 57.8 %all_to_all.21 = bf16[32,12,2048]{2,1,0:T(8,128)(2,1)S(1)} all-to-all(bf16[32,12,2048]{2,1,0:T(8,128)(2,1)S(1)} %select_convert_fusion), channel_id=1, replica_groups=mesh['dp'=8,'expert'=32] {'expert'}, dimensions={0} | all-to-all | bytes 3145728 | tf_op jit(solution)/shard_map/all_to_all | solution.py:97
  262.6 1.3 reshape.199
  264.0 4.1 convolution_convert_fusion
  268.3 2.3 multiply_convert_fusion.1
  270.6 2.4 convolution_convert_fusion.2
  273.0 2.4 convolution_convert_fusion.1
  275.4 21.4 %pad_maximum_fusion = bf16[2048,3072]{0,1:T(8,128)(2,1)} fusion(bf16[2048,1024]{0,1:T(8,128)(2,1)S(1)} %convolution_convert_fusion, bf16[2048,1024]{0,1:T(8,128)(2,1)S(1)} %convolution_convert_fusion.1, bf16[2048,1024]{0,1:T(8,128)(2,1)S(1)} %convolution_convert_fusion.2), kind=kLoop, calls=%fused_computation.6 | loop fusion | flops 37748736 | bytes 25165824 | tf_op jit(solution)/shard_map/concatenate | solution.py:118
  296.8 1.1 copy-done.17
  297.9 4.2 fusion.4
  302.1 1.8 add_convert_fusion
  303.9 1.5 reshape.200
  305.5 7.8 %all-to-all-start.3 = ((bf16[32,12,2048]{2,1,0:T(8,128)(2,1)}), bf16[32,12,2048]{2,1,0:T(8,128)(2,1)}, u32[]{:S(2)}, u32[]{:S(2)}) async-start(bf16[32,12,2048]{2,1,0:T(8,128)(2,1)} %reshape.200), calls=%async_computation.3 | async-start | bytes 4194304 | tf_op jit(solution)/shard_map/all_to_all | solution.py:113
  313.3 1.0 fusion.45
  314.4 2.6 copy_multiply_fusion
  317.0 43.3 %all-to-all-done.3 = bf16[32,12,2048]{2,1,0:T(8,128)(2,1)} async-done(((bf16[32,12,2048]{2,1,0:T(8,128)(2,1)}), bf16[32,12,2048]{2,1,0:T(8,128)(2,1)}, u32[]{:S(2)}, u32[]{:S(2)}) %all-to-all-start.3) | async-done | bytes 1572896 | tf_op jit(solution)/shard_map/all_to_all | solution.py:113
  360.3 2.7 reshape.201
  363.0 1.4 gather_fusion.4
  364.4 1.3 reshape.258
  365.8 1.6 fusion.44
  367.4 2.3 fusion.31
  369.7 74.9 %psum.15 = f32[2048]{0:T(1024)} all-reduce(f32[2048]{0:T(1024)S(1)} %get-tuple-element.35), channel_id=1, replica_groups=mesh['dp'=8,'expert'=32] {'dp','expert'}, use_global_device_ids=true, to_apply=%region_15.16 | all-reduce | flops 2048 | bytes 16384 | tf_op jit(solution)/shard_map/psum | solution.py:148
  444.7 2.7 fusion.30
  447.4 2.3 slice_bitcast_fusion.2
  449.7 1.0 copy.53
  450.7 1.0 copy.52
  451.7 178.7 %all-reduce.2.cloned.1.call-done = f32[2048,32]{0,1:T(8,128)} async-done(((f32[2048,32]{0,1:T(8,128)}), f32[2048,32]{0,1:T(8,128)}) %all-reduce.2.cloned.1.call-update) | async-done | bytes 262160 | tf_op jit(solution)/shard_map/psum | solution.py:148
  630.3 1.7 copy.66
  (70 shorter events, 1.1 us)
Async XLA Ops:
  7.2 141.4 %copy-start = (bf16[2048,32]{0,1:T(8,128)(2,1)S(1)}, bf16[2048,32]{0,1:T(8,128)(2,1)}, u32[]{:S(2)}) copy-start(bf16[2048,32]{0,1:T(8,128)(2,1)} %param.12) | copy-start | bytes 393220
  7.2 6.1 copy-start.3
  7.2 6.3 copy-start.10
  7.2 73.7 %all-gather.4.cloned.1.call-start = ((), (), s32[]{:S(2)}) async-start(), calls=%async_computation.5 | async-start | bytes 4718592 | tf_op jit(solution)/shard_map/all_gather | solution.py:67
  7.9 78.7 %all-gather.6.cloned.1.call-start = ((), (), s32[]{:S(2)}) async-start(), calls=%async_computation.6 | async-start | bytes 4718592 | tf_op jit(solution)/shard_map/all_gather | solution.py:68
  8.7 115.2 %all-gather.8.cloned.1.call-start = ((), (), s32[]{:S(2)}) async-start(), calls=%async_computation.7 | async-start | bytes 4718592 | tf_op jit(solution)/shard_map/all_gather | solution.py:78
  80.9 5.8 copy-start.7
  129.7 10.8 %copy-start.5 = (bf16[128,2048]{1,0:T(8,128)(2,1)S(1)}, bf16[128,2048]{1,0:T(8,128)(2,1)}, u32[]{:S(2)}) copy-start(bf16[128,2048]{1,0:T(8,128)(2,1)} %param.10) | copy-start | bytes 1572868
  129.7 58.4 %all-to-all-start.1 = ((bf16[32,12,2048]{2,1,0:T(8,128)(2,1)}), bf16[32,12,2048]{2,1,0:T(8,128)(2,1)}, u32[]{:S(2)}, u32[]{:S(2)}) async-start(bf16[32,12,2048]{2,1,0:T(8,128)(2,1)} %reshape.197), calls=%async_computation.1 | async-start | bytes 4194304 | tf_op jit(solution)/shard_map/all_to_all | solution.py:81
  140.0 307.4 %reduce-scatter.2.cloned.1.call-start = ((), (), s32[]{:S(2)}) async-start(), calls=%async_computation.8 | async-start | bytes 14155776 | tf_op jit(solution)/shard_map/reduce_scatter | solution.py:117
  143.9 4.9 copy-start.11
  264.0 4.2 copy-start.9
  264.0 4.2 copy-start.13
  264.0 4.2 copy-start.18
  264.0 4.3 copy-start.19
  268.3 2.3 copy-start.8
  270.5 2.4 copy-start.14
  270.6 2.4 copy-start.16
  296.8 1.1 copy-start.17
  297.9 4.2 copy-start.12
  297.9 4.2 copy-start.15
  305.5 8.9 %copy-start.1 = (f32[128,2,2048]{2,1,0:T(2,128)S(1)}, f32[128,2,2048]{2,1,0:T(2,128)}, u32[]{:S(2)}) copy-start(f32[128,2,2048]{2,1,0:T(2,128)} %reshape.257) | copy-start | bytes 6291460
  305.5 54.9 %all-to-all-start.3 = ((bf16[32,12,2048]{2,1,0:T(8,128)(2,1)}), bf16[32,12,2048]{2,1,0:T(8,128)(2,1)}, u32[]{:S(2)}, u32[]{:S(2)}) async-start(bf16[32,12,2048]{2,1,0:T(8,128)(2,1)} %reshape.200), calls=%async_computation.3 | async-start | bytes 4194304 | tf_op jit(solution)/shard_map/all_to_all | solution.py:113
  313.3 317.1 %all-reduce.2.cloned.1.call-start = ((), (), s32[]{:S(2)}) async-start(), calls=%async_computation.9 | async-start | bytes 524288 | tf_op jit(solution)/shard_map/psum | solution.py:148
  365.8 1.7 copy-start.4
  367.4 77.3 %copy-start.2 = (f32[128,2,2048]{2,0,1:T(8,128)S(1)}, f32[128,2,2048]{2,0,1:T(8,128)}, u32[]{:S(2)}) copy-start(f32[128,2,2048]{2,0,1:T(8,128)} %copy_multiply_fusion) | copy-start | bytes 6291460
  367.4 77.3 %copy-start.6 = (bf16[128,2048]{1,0:T(8,128)(2,1)S(1)}, bf16[128,2048]{1,0:T(8,128)(2,1)}, u32[]{:S(2)}) copy-start(bf16[128,2048]{1,0:T(8,128)(2,1)} %param.10) | copy-start | bytes 1572868
Sparse Core Ops, SparseCore 0:
  9.9 37.5 all-gather.3
  49.3 34.5 all-gather.5
  85.8 38.0 all-gather.7
  296.9 73.3 reduce-scatter.1
  376.2 254.0 all-reduce.1
where the time goes:
time: 646 us; the launch traced here: 639 us
  waiting for transfers between devices  295 us (46%)
  blocking collectives  193 us (30%)
  local copies, waits for them, and re-layouts  48 us (7%)
  matrix products  36.7 us (6%)
  other arithmetic  33.7 us (5%)
  starting transfers between devices  18.6 us (3%)
  between operations  14.5 us (2%)
    psum x1, waiting for transfers between devices, on_device(): d_router, d_gain = lax.psum((part_router, part_gain), ('dp', 'expert'))  179 us
    psum x1, blocking collectives, on_device(): d_router, d_gain = lax.psum((part_router, part_gain), ('dp', 'expert'))  74.9 us
    all_to_all x1, blocking collectives, on_device(): lax.all_to_all(send_rows.reshape(experts, capacity, width), 'expert', spl...  60 us
    all_to_all x1, blocking collectives, on_device(): lax.all_to_all(d_send.reshape(experts, capacity, width), 'expert', split_...  57.8 us
    all_to_all x1, waiting for transfers between devices, on_device(): lax.all_to_all(d_rows.reshape(experts, capacity, width), 'expert', split_...  43.3 us
    all_to_all x1, waiting for transfers between devices, on_device(): lax.all_to_all(expert_out.reshape(experts, capacity, width), 'expert', sp...  39.2 us
    all_gather x1, waiting for transfers between devices, on_device(): lax.all_gather(down_weight, 'dp', axis=2, tiled=True)[0]  31.3 us
    concatenate x1, other arithmetic, on_device(): jnp.concatenate([inner_product(expert_in, d_pre_gate), inner_product(expe...  21.4 us
  transfers between devices with their start and end apart: 7, of which 4 were waited for; matrix products, arithmetic and copies ran while one was open for 9% of the time, Pallas kernels for 0%

commit v1 on v0

v1 whole, which is shorter than its diff:
```python
import jax
import jax.numpy as jnp
from jax import lax
from jax.sharding import PartitionSpec as P

norm_eps = 1e-06
f32 = jnp.float32
bf16 = jnp.bfloat16


def dot(left, right, dims, **options):
    return lax.dot_general(
        left, right, (dims, ((), ())), preferred_element_type=f32, **options
    )


def exchange(rows, experts):
    count, width = rows.shape
    packed = rows.reshape(experts, count // experts, width // 128, 128)
    moved = lax.all_to_all(packed, "expert", split_axis=0, concat_axis=0, tiled=True)
    return moved.reshape(count, width)


def on_device(
    tokens, expert_ids, upstream, gain, router, gate_weight_matrix, up_weight, down_weight
):
    experts = lax.axis_size("expert")
    tok_rows, width = tokens.shape
    capacity = 3 * tok_rows // experts
    slots = experts * capacity

    gate_full = lax.all_gather(gate_weight_matrix[0], "dp", axis=0, tiled=True)
    up_full = lax.all_gather(up_weight[0], "dp", axis=0, tiled=True)
    down_full = lax.all_gather(down_weight[0], "dp", axis=1, tiled=True)

    columns = jnp.arange(experts, dtype=jnp.int32)
    picked = expert_ids[:, :, None] == columns[None, None, :]
    named = (picked[:, 0] | picked[:, 1]).astype(bf16)
    order = jnp.arange(tok_rows, dtype=jnp.int32)
    earlier = (order[None, :] < order[:, None]).astype(bf16)
    ranks = dot(earlier, named, ((1,), (0,))).astype(jnp.int32)
    place = columns[None, :] * capacity + ranks
    slot_pairs = jnp.sum(jnp.where(picked, place[:, None, :], 0), axis=2)
    slot_of = jnp.arange(slots, dtype=jnp.int32)
    first = slot_of[None, :] == slot_pairs[:, :1]
    second = slot_of[None, :] == slot_pairs[:, 1:]
    take_first = first.astype(bf16)
    take_second = second.astype(bf16)
    spread = (first | second).astype(bf16)

    source = tokens.astype(f32)
    inverse = lax.rsqrt(jnp.mean(source * source, axis=-1, keepdims=True) + norm_eps)
    unit_rows = source * inverse
    normed = (unit_rows * gain).astype(bf16)
    send_rows = dot(spread, normed, ((0,), (0,))).astype(bf16)
    expert_in = exchange(send_rows, experts)

    scores = jax.nn.sigmoid(jnp.dot(normed, router, preferred_element_type=f32))
    chosen = jnp.sum(jnp.where(picked, scores[:, None, :], 0.0), axis=2)
    total = jnp.sum(chosen, axis=1, keepdims=True)
    gates = chosen / total
    slot_gates = jnp.sum(
        jnp.where(first, gates[:, :1], 0.0) + jnp.where(second, gates[:, 1:], 0.0), axis=0
    )
    cot_rows = dot(spread, upstream, ((0,), (0,)))
    d_send = (slot_gates[:, None] * cot_rows).astype(bf16)
    d_send, expert_in = lax.optimization_barrier((d_send, expert_in))
    d_out = exchange(d_send, experts)

    pre_gate = dot(expert_in, gate_full, ((1,), (0,)))
    pre_up = dot(expert_in, up_full, ((1,), (0,)))
    sigma = jax.nn.sigmoid(pre_gate)
    active = pre_gate * sigma
    hidden = (active * pre_up).astype(bf16)
    expert_out = dot(hidden, down_full, ((1,), (0,))).astype(bf16)
    returned = exchange(expert_out, experts)

    d_out, hidden, expert_out = lax.optimization_barrier((d_out, hidden, expert_out))
    down_part = dot(d_out, hidden, ((0,), (0,))).astype(bf16)
    d_down = lax.psum_scatter(down_part, "dp", scatter_dimension=0, tiled=True)
    d_out, down_part = lax.optimization_barrier((d_out, down_part))
    d_hidden = dot(d_out, down_full, ((1,), (1,)))
    d_pre_gate = (d_hidden * pre_up * sigma * (1.0 + pre_gate * (1.0 - sigma))).astype(bf16)
    d_pre_up = (d_hidden * active).astype(bf16)
    d_rows = (
        dot(d_pre_gate, gate_full, ((1,), (1,))) + dot(d_pre_up, up_full, ((1,), (1,)))
    ).astype(bf16)
    d_back = exchange(d_rows, experts)
    d_pre_gate, d_pre_up, d_rows = lax.optimization_barrier((d_pre_gate, d_pre_up, d_rows))
    d_gate = lax.psum_scatter(
        dot(expert_in, d_pre_gate, ((0,), (0,))).astype(bf16),
        "dp",
        scatter_dimension=0,
        tiled=True,
    )
    d_up = lax.psum_scatter(
        dot(expert_in, d_pre_up, ((0,), (0,))).astype(bf16),
        "dp",
        scatter_dimension=0,
        tiled=True,
    )
    gain_rows = jnp.sum(d_rows.astype(f32) * expert_in.astype(f32), axis=0) / gain

    cotangent = upstream.astype(f32)
    out_first = dot(take_first, returned, ((1,), (0,)))
    out_second = dot(take_second, returned, ((1,), (0,)))
    mixed = (source + gates[:, :1] * out_first + gates[:, 1:] * out_second).astype(bf16)
    d_gates = jnp.concatenate(
        [
            jnp.sum(cotangent * out_first, axis=1, keepdims=True),
            jnp.sum(cotangent * out_second, axis=1, keepdims=True),
        ],
        axis=1,
    )
    blended = jnp.sum(gates * d_gates, axis=1, keepdims=True)
    d_chosen = (d_gates - blended) / total
    d_logit = d_chosen * chosen * (1.0 - chosen)
    d_logits = jnp.sum(jnp.where(picked, d_logit[:, :, None], 0.0), axis=1)
    d_scored = dot(
        d_logits, router.astype(f32), ((1,), (1,)), precision=lax.Precision.HIGHEST
    )

    part_router = dot(
        d_logits, normed.astype(f32), ((0,), (0,)), precision=lax.Precision.HIGHEST
    )
    part_gain = gain_rows + jnp.sum(d_scored * unit_rows, axis=0)
    piece = width // experts
    parts = jnp.concatenate(
        [part_router, jnp.pad(part_gain.reshape(experts, piece), ((0, 0), (0, 128 - piece)))],
        axis=1,
    )
    mine = lax.all_to_all(parts[:, None], "expert", split_axis=0, concat_axis=0, tiled=True)
    mine = lax.psum(jnp.sum(mine, axis=0), "dp")
    every = lax.all_to_all(
        jnp.broadcast_to(mine[None], (experts,) + mine.shape),
        "expert",
        split_axis=0,
        concat_axis=0,
        tiled=True,
    )[:, 0]
    d_back, every = lax.optimization_barrier((d_back, every))
    d_router = every[:, :width].T
    d_gain = every[:, width : width + piece].reshape(width)

    spread_all = dot(spread, d_back, ((1,), (0,)))
    d_normed = spread_all + d_scored
    d_unit = d_normed * gain
    inner = jnp.mean(d_unit * unit_rows, axis=-1, keepdims=True)
    d_tokens = (cotangent + inverse * (d_unit - unit_rows * inner)).astype(bf16)
    return (
        mixed,
        d_tokens,
        d_gate[None],
        d_up[None],
        d_down.T[None],
        d_router,
        d_gain,
    )


def solution(mesh):
    return jax.shard_map(
        on_device,
        mesh=mesh,
        in_specs=(
            P(("dp", "expert"), None),
            P(("dp", "expert"), None),
            P(("dp", "expert"), None),
            P(),
            P(),
            P("expert", "dp", None),
            P("expert", "dp", None),
            P("expert", None, "dp"),
        ),
        out_specs=(
            P(("dp", "expert"), None),
            P(("dp", "expert"), None),
            P("expert", "dp", None),
            P("expert", "dp", None),
            P("expert", None, "dp"),
            P(),
            P(),
        ),
        check_vma=False,
    )
```

time: 646 us -> 304 us (0.47)
  waiting for transfers between devices: 295 us -> 96.4 us
  blocking collectives: 193 us -> 70 us
  other arithmetic: 33.7 us -> 4.46 us
  local copies, waits for them, and re-layouts: 48 us -> 19.3 us
  starting transfers between devices: 18.6 us -> 44.5 us
  matrix products: 36.7 us -> 53 us
    psum x1 -> x0, waiting for transfers between devices: 179 us -> none  [on_device(): d_router, d_gain = lax.psum((part_router, part_gain), ('dp', 'expert'))]
    all_to_all x2 -> x1, blocking collectives: 118 us -> 45.2 us  [exchange(): lax.all_to_all(packed, 'expert', split_axis=0, concat_axis=0, tiled=True)]
    psum x1, blocking collectives: 74.9 us -> 24.8 us  [on_device(): mine = lax.psum(jnp.sum(mine, axis=0), 'dp')]
    all_gather x3, waiting for transfers between devices: 31.3 us -> 1.37 us  [the longest x1 1.36 us: on_device(): down_full = lax.all_gather(down_weight[0], 'dp', axis=1, tiled=True)]
    all_to_all x2 -> x5, starting transfers between devices: 18.1 us -> 43.8 us  [the longest x3 27.6 us: exchange(): lax.all_to_all(packed, 'expert', split_axis=0, concat_axis=0, tiled=True)]
    concatenate x1 -> x0, other arithmetic: 21.4 us -> none  [on_device(): jnp.concatenate([inner_product(expert_in, d_pre_gate), inner_product(expe...]
    gather x7 -> x0, local copies, waits for them, and re-layouts: 19.9 us -> none  [the longest x2 7.9 us: on_device(): cotangent[sources // 2]]
    dot_general x12 -> x18, matrix products: 36.7 us -> 53 us  [the longest x17 52.6 us: dot(): lax.dot_general(left, right, (dims, ((), ())), preferred_element_type=f32...]
  transfers between devices with their start and end apart: 7 -> 11, of which waited for: 4 -> 6; matrix products, arithmetic and copies ran while one was open for 9% -> 22% of each run, Pallas kernels for 0% -> 0%
where the time goes in v1:
time: 304 us; the launch traced here: 302 us
  waiting for transfers between devices  96.4 us (32%)
  blocking collectives  70 us (23%)
  matrix products  53 us (17%)
  starting transfers between devices  44.5 us (15%)
  local copies, waits for them, and re-layouts  19.3 us (6%)
  between operations  14.5 us (5%)
  other arithmetic  4.46 us (1%)
    all_to_all x3, waiting for transfers between devices, exchange(): lax.all_to_all(packed, 'expert', split_axis=0, concat_axis=0, tiled=True)  74.1 us
    dot_general x17, matrix products, dot(): lax.dot_general(left, right, (dims, ((), ())), preferred_element_type=f32...  52.6 us
    all_to_all x1, blocking collectives, exchange(): lax.all_to_all(packed, 'expert', split_axis=0, concat_axis=0, tiled=True)  45.2 us
    all_to_all x3, starting transfers between devices, exchange(): lax.all_to_all(packed, 'expert', split_axis=0, concat_axis=0, tiled=True)  27.6 us
    psum x1, blocking collectives, on_device(): mine = lax.psum(jnp.sum(mine, axis=0), 'dp')  24.8 us
    unnamed x45, local copies, waits for them, and re-layouts  16 us
    all_to_all x1, waiting for transfers between devices, on_device(): lax.all_to_all(parts[:, None], 'expert', split_axis=0, concat_axis=0, til...  9.74 us
    all_to_all x1, waiting for transfers between devices, on_device(): lax.all_to_all(jnp.broadcast_to(mine[None], (experts,) + mine.shape), 'ex...  9.15 us
  transfers between devices with their start and end apart: 11, of which 6 were waited for; matrix products, arithmetic and copies ran while one was open for 22% of the time, Pallas kernels for 0%

profile of v1, /device:TPU:2, one launch (start us, length us, event | category | flops | bytes accessed | tf_op | source)
XLA Modules:
  0.0 302.1 jit_solution(15065275371756524959)
XLA Ops:
  7.2 0.0 all-gather.7.cloned.1.call-start
  7.3 0.7 all-gather.7.cloned.1.call-update
  7.9 0.0 all-gather.9.cloned.1.call-start
  8.0 0.7 all-gather.9.cloned.1.call-update
  8.7 0.0 all-gather.11.cloned.1.call-start
  8.7 0.7 all-gather.11.cloned.1.call-update
  9.5 0.2 fusion.39
  9.7 0.1 fusion.30
  9.8 0.1 select_reduce_fusion.3
  9.9 0.7 fusion.27
  10.6 1.6 copy.26
  12.2 11.7 %all-to-all-start = ((bf16[32,12,16,128]{3,2,1,0:T(8,128)(2,1)}), bf16[32,12,16,128]{3,2,1,0:T(8,128)(2,1)S(1)}, u32[]{:S(2)}, u32[]{:S(2)}) async-start(bf16[32,12,16,128]{3,2,1,0:T(8,128)(2,1)} %bitcast.110), calls=%async_computation | async-start | bytes 3145728 | tf_op jit(solution)/shard_map/all_to_all | solution.py:20
  24.0 0.0 reduce-scatter.8.cloned.1.call-start
  24.0 0.4 fusion.33
  24.5 0.1 add_reduce_fusion
  24.6 1.9 multiply_convert_fusion
  26.5 34.3 %all-to-all-done = bf16[32,12,16,128]{3,2,1,0:T(8,128)(2,1)S(1)} async-done(((bf16[32,12,16,128]{3,2,1,0:T(8,128)(2,1)}), bf16[32,12,16,128]{3,2,1,0:T(8,128)(2,1)S(1)}, u32[]{:S(2)}, u32[]{:S(2)}) %all-to-all-start) | async-done | bytes 1572896 | tf_op jit(solution)/shard_map/all_to_all | solution.py:20
  60.8 1.2 copy-done.3
  62.0 2.2 copy.50
  64.2 0.4 copy.28
  64.7 45.2 %all_to_all.30 = bf16[32,12,16,128]{3,2,1,0:T(8,128)(2,1)S(1)} all-to-all(bf16[32,12,16,128]{3,2,1,0:T(8,128)(2,1)S(1)} %bitcast.115), channel_id=1, replica_groups=mesh['dp'=8,'expert'=32] {'expert'}, dimensions={0} | all-to-all | bytes 3145728 | tf_op jit(solution)/shard_map/all_to_all | solution.py:20
  109.9 1.6 copy.49
  111.4 5.1 %fusion.10 = f32[384,1024]{1,0:T(8,128)} fusion(bf16[384,2048]{1,0:T(8,128)(2,1)S(1)} %bitcast.103, bf16[1,2048,1024]{2,1,0:T(8,128)(2,1)} %all-gather.7.cloned.1.call-done), kind=kOutput, calls=%fused_computation.10 | convolution fusion | flops 1610612736 | bytes 7340032 | tf_op jit(solution)/shard_map/dot_general | solution.py:12
  116.6 6.0 %multiply_convert_fusion.3 = (bf16[384,1024]{1,0:T(8,128)(2,1)}, f32[384,1024]{1,0:T(8,128)}) fusion(f32[384,1024]{1,0:T(8,128)} %fusion.10, bf16[384,2048]{1,0:T(8,128)(2,1)S(1)} %bitcast.104, bf16[1,2048,1024]{2,1,0:T(8,128)(2,1)} %all-gather.9.cloned.1.call-done), kind=kOutput, calls=%fused_computation.34 | convolution fusion | flops 1612972032 | bytes 9699328 | tf_op jit(solution)/shard_map/dot_general | solution.py:12
  122.6 1.4 all-gather.11.cloned.1.call-done
  123.9 5.5 %fusion.14 = bf16[384,2048]{1,0:T(8,128)(2,1)} fusion(bf16[384,1024]{1,0:T(8,128)(2,1)} %get-tuple-element.20, bf16[1,1024,2048]{2,1,0:T(8,128)(2,1)} %all-gather.11.cloned.1.call-done), kind=kOutput, calls=%fused_computation.18 | convolution fusion | flops 1611399168 | bytes 6553600 | tf_op jit(solution)/shard_map/dot_general | solution.py:12
  129.5 4.4 %convolution_convert_fusion.2 = bf16[2048,1024]{1,0:T(8,128)(2,1)} fusion(bf16[384,2048]{1,0:T(8,128)(2,1)S(1)} %bitcast.120, bf16[384,1024]{1,0:T(8,128)(2,1)S(1)} %copy-done.17), kind=kOutput, calls=%fused_computation.14 | convolution fusion | flops 1612709888 | bytes 6553600 | tf_op jit(solution)/shard_map/dot_general | solution.py:12
  133.8 0.0 reduce-scatter.8.cloned.1.call-update
  133.9 0.2 reduce-scatter.6.cloned.1.call-start
  134.1 5.9 %multiply_convert_fusion.2 = (bf16[384,1024]{1,0:T(8,128)(2,1)S(1)}, bf16[384,1024]{1,0:T(8,128)(2,1)S(1)}) fusion(f32[384,1024]{1,0:T(8,128)} %fusion.10, f32[384,1024]{1,0:T(8,128)} %get-tuple-element.67, bf16[384,2048]{1,0:T(8,128)(2,1)} %bitcast.119, bf16[1,1024,2048]{2,1,0:T(8,128)(2,1)} %all-gather.11.cloned.1.call-done), kind=kOutput, calls=%fused_computation.30 | convolution fusion | flops 1615724544 | bytes 10485760 | tf_op jit(solution)/shard_map/dot_general | solution.py:12
  140.1 1.8 fusion.4
  141.9 0.6 copy-done.14
  142.5 3.0 %add_convert_fusion = bf16[384,2048]{1,0:T(8,128)(2,1)} fusion(f32[384,2048]{1,0:T(8,128)S(1)} %fusion.4, bf16[384,1024]{1,0:T(8,128)(2,1)S(1)} %get-tuple-element.24, bf16[1,2048,1024]{2,1,0:T(8,128)(2,1)S(1)} %copy-done.14), kind=kOutput, calls=%fused_computation.16 | convolution fusion | flops 1612185600 | bytes 9699328 | tf_op jit(solution)/shard_map/dot_general | solution.py:12
  145.6 4.3 %convolution_convert_fusion = bf16[2048,1024]{1,0:T(8,128)(2,1)} fusion(bf16[384,2048]{1,0:T(8,128)(2,1)S(1)} %bitcast.105, bf16[384,1024]{1,0:T(8,128)(2,1)S(1)} %get-tuple-element.25), kind=kOutput, calls=%fused_computation.12 | convolution fusion | flops 1612709888 | bytes 6553600 | tf_op jit(solution)/shard_map/dot_general | solution.py:12
  149.9 0.0 reduce-scatter.6.cloned.1.call-update
  149.9 3.0 copy.30
  152.9 10.2 %all-to-all-start.1 = ((bf16[32,12,16,128]{3,2,1,0:T(8,128)(2,1)}), bf16[32,12,16,128]{3,2,1,0:T(8,128)(2,1)}, u32[]{:S(2)}, u32[]{:S(2)}) async-start(bf16[32,12,16,128]{3,2,1,0:T(8,128)(2,1)} %bitcast.112), calls=%async_computation.1 | async-start | bytes 3145728 | tf_op jit(solution)/shard_map/all_to_all | solution.py:20
  163.1 0.3 reduce-scatter.4.cloned.1.call-start
  163.4 5.5 %convolution_convert_fusion.1 = bf16[2048,1024]{1,0:T(8,128)(2,1)} fusion(bf16[384,2048]{1,0:T(8,128)(2,1)S(1)} %bitcast.106, bf16[384,1024]{1,0:T(8,128)(2,1)} %copy-done.16), kind=kOutput, calls=%fused_computation.13 | convolution fusion | flops 1612709888 | bytes 6553600 | tf_op jit(solution)/shard_map/dot_general | solution.py:12
  168.9 0.0 reduce-scatter.4.cloned.1.call-update
  168.9 1.9 multiply_reduce_fusion
  170.8 29.5 %all-to-all-done.1 = bf16[32,12,16,128]{3,2,1,0:T(8,128)(2,1)} async-done(((bf16[32,12,16,128]{3,2,1,0:T(8,128)(2,1)}), bf16[32,12,16,128]{3,2,1,0:T(8,128)(2,1)}, u32[]{:S(2)}, u32[]{:S(2)}) %all-to-all-start.1) | async-done | bytes 1572896 | tf_op jit(solution)/shard_map/all_to_all | solution.py:20
  200.3 1.9 fusion.18
  202.2 3.1 %fusion.42 = (f32[128]{0:T(128)S(1)}, f32[128]{0:T(128)S(1)}, bf16[128,2048]{1,0:T(8,128)(2,1)}) fusion(bf16[128,2048]{1,0:T(8,128)(2,1)S(1)} %copy-done.5, f32[128,2048]{1,0:T(8,128)S(1)} %fusion.18, f32[128]{0:T(128)S(1)} %get-tuple-element.65, f32[128]{0:T(128)S(1)} %get-tuple-element.64, bf16[128,2048]{1,0:T(8,128)(2,1)S(1)} %copy-done.1, ...), kind=kOutput, calls=%fused_computation.61 | convolution fusion | flops 204259072 | bytes 4196864 | tf_op jit(solution)/shard_map/dot_general | solution.py:12
  205.4 0.7 fusion.35
  206.1 0.1 reshape.131
  206.2 0.5 fusion.62
  206.7 1.0 copy.23
  207.7 8.3 %all-to-all-start.4 = ((f32[32,1,2176]{2,1,0:T(1,128)}), f32[32,1,2176]{2,1,0:T(1,128)S(1)}, u32[]{:S(2)}, u32[]{:S(2)}) async-start(f32[32,1,2176]{2,1,0:T(1,128)} %copy.23), calls=%async_computation.4 | async-start | bytes 557056 | tf_op jit(solution)/shard_map/all_to_all | solution.py:132
  216.0 1.6 copy.32
  217.6 9.7 %all-to-all-done.4 = f32[32,1,2176]{2,1,0:T(1,128)S(1)} async-done(((f32[32,1,2176]{2,1,0:T(1,128)}), f32[32,1,2176]{2,1,0:T(1,128)S(1)}, u32[]{:S(2)}, u32[]{:S(2)}) %all-to-all-start.4) | async-done | bytes 278560 | tf_op jit(solution)/shard_map/all_to_all | solution.py:132
  227.3 5.7 %all-to-all-start.3 = ((bf16[32,12,16,128]{3,2,1,0:T(8,128)(2,1)}), bf16[32,12,16,128]{3,2,1,0:T(8,128)(2,1)S(1)}, u32[]{:S(2)}, u32[]{:S(2)}) async-start(bf16[32,12,16,128]{3,2,1,0:T(8,128)(2,1)} %bitcast.113), calls=%async_computation.3 | async-start | bytes 3145728 | tf_op jit(solution)/shard_map/all_to_all | solution.py:20
  233.0 0.8 reduce_sum.130
  233.8 24.8 %psum.7 = f32[2176]{0:T(1024)S(1)} all-reduce(f32[2176]{0:T(1024)} %reduce_sum.130), channel_id=1, replica_groups=mesh['dp'=8,'expert'=32] {'dp'}, use_global_device_ids=true, to_apply=%region_12.13 | all-reduce | flops 2176 | bytes 17408 | tf_op jit(solution)/shard_map/psum | solution.py:133
  258.6 10.3 %all-to-all-done.3 = bf16[32,12,16,128]{3,2,1,0:T(8,128)(2,1)S(1)} async-done(((bf16[32,12,16,128]{3,2,1,0:T(8,128)(2,1)}), bf16[32,12,16,128]{3,2,1,0:T(8,128)(2,1)S(1)}, u32[]{:S(2)}, u32[]{:S(2)}) %all-to-all-start.3) | async-done | bytes 1572896 | tf_op jit(solution)/shard_map/all_to_all | solution.py:20
  268.9 0.9 broadcast_in_dim.104
  269.8 7.9 %all-to-all-start.5 = ((f32[32,1,2176]{2,1,0:T(1,128)}), f32[32,1,2176]{2,1,0:T(1,128)S(1)}, u32[]{:S(2)}, u32[]{:S(2)}) async-start(f32[32,1,2176]{2,1,0:T(1,128)} %broadcast_in_dim.104), calls=%async_computation.5 | async-start | bytes 557056 | tf_op jit(solution)/shard_map/all_to_all | solution.py:134
  277.7 1.6 copy.48
  279.3 9.1 %all-to-all-done.5 = f32[32,1,2176]{2,1,0:T(1,128)S(1)} async-done(((f32[32,1,2176]{2,1,0:T(1,128)}), f32[32,1,2176]{2,1,0:T(1,128)S(1)}, u32[]{:S(2)}, u32[]{:S(2)}) %all-to-all-start.5) | async-done | bytes 278560 | tf_op jit(solution)/shard_map/all_to_all | solution.py:134
  288.5 0.7 reshape.132
  289.2 2.1 fusion.36
  291.3 0.7 slice_bitcast_fusion
  292.0 1.2 fusion.44
  293.2 2.0 copy.24
  (54 shorter events, 0.3 us)
Async XLA Ops:
  7.2 16.9 %copy-start = (bf16[2048,32]{0,1:T(8,128)(2,1)S(1)}, bf16[2048,32]{0,1:T(8,128)(2,1)}, u32[]{:S(2)}) copy-start(bf16[2048,32]{0,1:T(8,128)(2,1)} %param.12) | copy-start | bytes 393220
  7.2 2.3 copy-start.1
  7.2 2.5 copy-start.10
  7.2 2.7 copy-start.8
  7.2 104.2 %all-gather.7.cloned.1.call-start = ((), (), s32[]{:S(2)}) async-start(), calls=%async_computation.12 | async-start | bytes 4718592 | tf_op jit(solution)/shard_map/all_gather | solution.py:32
  7.9 108.6 %all-gather.9.cloned.1.call-start = ((), (), s32[]{:S(2)}) async-start(), calls=%async_computation.13 | async-start | bytes 4718592 | tf_op jit(solution)/shard_map/all_gather | solution.py:33
  8.7 115.2 %all-gather.11.cloned.1.call-start = ((), (), s32[]{:S(2)}) async-start(), calls=%async_computation.14 | async-start | bytes 4718592 | tf_op jit(solution)/shard_map/all_gather | solution.py:34
  9.7 196.5 %copy-start.12 = (f32[128]{0:T(128)}, f32[128]{0:T(128)S(1)}, u32[]{:S(2)}) copy-start(f32[128]{0:T(128)S(1)} %add_rsqrt_fusion) | copy-start | bytes 1540
  9.9 190.5 %copy-start.9 = (s32[128]{0:T(128)}, s32[128]{0:T(128)S(1)}, u32[]{:S(2)}) copy-start(s32[128]{0:T(128)S(1)} %get-tuple-element.63) | copy-start | bytes 1540
  9.9 192.3 %copy-start.11 = (s32[128]{0:T(128)}, s32[128]{0:T(128)S(1)}, u32[]{:S(2)}) copy-start(s32[128]{0:T(128)S(1)} %get-tuple-element.62) | copy-start | bytes 1540
  12.2 12.4 %copy-start.5 = (bf16[128,2048]{1,0:T(8,128)(2,1)S(1)}, bf16[128,2048]{1,0:T(8,128)(2,1)}, u32[]{:S(2)}) copy-start(bf16[128,2048]{1,0:T(8,128)(2,1)} %param.10) | copy-start | bytes 1572868
  12.2 48.6 %all-to-all-start = ((bf16[32,12,16,128]{3,2,1,0:T(8,128)(2,1)}), bf16[32,12,16,128]{3,2,1,0:T(8,128)(2,1)S(1)}, u32[]{:S(2)}, u32[]{:S(2)}) async-start(bf16[32,12,16,128]{3,2,1,0:T(8,128)(2,1)} %bitcast.110), calls=%async_computation | async-start | bytes 3145728 | tf_op jit(solution)/shard_map/all_to_all | solution.py:20
  24.0 269.3 %reduce-scatter.8.cloned.1.call-start = ((), (), s32[]{:S(2)}) async-start(), calls=%async_computation.11 | async-start | bytes 4718592 | tf_op jit(solution)/shard_map/reduce_scatter | solution.py:80
  60.8 1.2 copy-start.3
  62.0 2.3 copy-start.4
  123.9 5.5 %copy-start.7 = (bf16[48,8,16,128]{3,1,2,0:T(8,128)(2,1)S(1)}, bf16[48,8,16,128]{3,1,2,0:T(8,128)(2,1)}, u32[]{:S(2)}) copy-start(bf16[48,8,16,128]{3,1,2,0:T(8,128)(2,1)} %copy.49) | copy-start | bytes 4718596
  123.9 5.5 %copy-start.17 = (bf16[384,1024]{1,0:T(8,128)(2,1)S(1)}, bf16[384,1024]{1,0:T(8,128)(2,1)}, u32[]{:S(2)}) copy-start(bf16[384,1024]{1,0:T(8,128)(2,1)} %get-tuple-element.20) | copy-start | bytes 2359300
  133.9 161.4 %reduce-scatter.6.cloned.1.call-start = ((), (), s32[]{:S(2)}) async-start(), calls=%async_computation.10 | async-start | bytes 4718592 | tf_op jit(solution)/shard_map/reduce_scatter | solution.py:96
  134.1 6.0 %copy-start.15 = (bf16[1,2048,1024]{2,1,0:T(8,128)(2,1)S(1)}, bf16[1,2048,1024]{2,1,0:T(8,128)(2,1)}, u32[]{:S(2)}) copy-start(bf16[1,2048,1024]{2,1,0:T(8,128)(2,1)} %all-gather.9.cloned.1.call-done) | copy-start | bytes 12582916
  140.0 1.9 copy-start.16
  140.1 2.5 copy-start.14
  152.9 47.4 %all-to-all-start.1 = ((bf16[32,12,16,128]{3,2,1,0:T(8,128)(2,1)}), bf16[32,12,16,128]{3,2,1,0:T(8,128)(2,1)}, u32[]{:S(2)}, u32[]{:S(2)}) async-start(bf16[32,12,16,128]{3,2,1,0:T(8,128)(2,1)} %bitcast.112), calls=%async_computation.1 | async-start | bytes 3145728 | tf_op jit(solution)/shard_map/all_to_all | solution.py:20
  163.1 132.2 %reduce-scatter.4.cloned.1.call-start = ((), (), s32[]{:S(2)}) async-start(), calls=%async_computation.9 | async-start | bytes 4718592 | tf_op jit(solution)/shard_map/reduce_scatter | solution.py:90
  206.1 9.9 %copy-start.2 = (bf16[384,2048]{1,0:T(8,128)(2,1)S(1)}, bf16[384,2048]{1,0:T(8,128)(2,1)}, u32[]{:S(2)}) copy-start(bf16[384,2048]{1,0:T(8,128)(2,1)} %add_convert_fusion) | copy-start | bytes 4718596
  207.7 19.6 %all-to-all-start.4 = ((f32[32,1,2176]{2,1,0:T(1,128)}), f32[32,1,2176]{2,1,0:T(1,128)S(1)}, u32[]{:S(2)}, u32[]{:S(2)}) async-start(f32[32,1,2176]{2,1,0:T(1,128)} %copy.23), calls=%async_computation.4 | async-start | bytes 557056 | tf_op jit(solution)/shard_map/all_to_all | solution.py:132
  227.3 41.6 %all-to-all-start.3 = ((bf16[32,12,16,128]{3,2,1,0:T(8,128)(2,1)}), bf16[32,12,16,128]{3,2,1,0:T(8,128)(2,1)S(1)}, u32[]{:S(2)}, u32[]{:S(2)}) async-start(bf16[32,12,16,128]{3,2,1,0:T(8,128)(2,1)} %bitcast.113), calls=%async_computation.3 | async-start | bytes 3145728 | tf_op jit(solution)/shard_map/all_to_all | solution.py:20
  269.8 18.7 %all-to-all-start.5 = ((f32[32,1,2176]{2,1,0:T(1,128)}), f32[32,1,2176]{2,1,0:T(1,128)S(1)}, u32[]{:S(2)}, u32[]{:S(2)}) async-start(f32[32,1,2176]{2,1,0:T(1,128)} %broadcast_in_dim.104), calls=%async_computation.5 | async-start | bytes 557056 | tf_op jit(solution)/shard_map/all_to_all | solution.py:134
  289.2 2.9 copy-start.6
  289.2 2.9 copy-start.13
Sparse Core Ops, SparseCore 0:
  9.9 37.5 all-gather.6
  49.3 34.6 all-gather.8
  85.8 38.0 all-gather.10
  134.0 41.7 reduce-scatter.7
  178.8 40.0 reduce-scatter.5
  221.8 40.2 reduce-scatter.3
